TPU v7x, 1024 devices: a whole 4x8x16 slice. The times are simulated.
1024 devices in a mesh: row: 64 (over z, x), col: 16 (over y, core).
Axes of the slice: x: 4, y: 8, z: 16, core: 2. Of those that a mesh axis runs over, the one named last changes fastest.
Arguments:
- matrix: float32 [16384, 16384], P('row', 'col'), as said below
Outputs:
- factored: float32 [16384, 16384], P('row', 'col')
Inputs may be any that keep to these rules, and one draw needn't show every extreme that they name: `matrix`: each diagonal entry lies between 3 and 6 times the square root of 256; every other entry has magnitude 6 or less.
All inputs are finite; a program needn't handle non-finite values.
Results may differ from a plain program's by a relative error of at most 0.00085.
Values may be sent and summed in bfloat16 or wider, within the bound.
A program may use at most 32 MiB of HBM per device.

v0:
```python
import jax
import jax.numpy as jnp
from jax import lax
from jax.sharding import PartitionSpec as P

NB = 256
SWEEPS = 2


def broadcast(value, axis, source):
    kept = jnp.where(lax.axis_index(axis) == source, value, 0).astype(value.dtype)
    return lax.psum(kept, axis)


def newton(square):
    size = square.shape[0]
    identity = jnp.eye(size, dtype=jnp.float32)
    approx = identity / jnp.diagonal(square)[None, :]
    for sweep in range(SWEEPS):
        product = jnp.dot(square, approx, precision=lax.Precision.HIGHEST)
        approx = jnp.dot(approx, 2.0 * identity - product, precision=lax.Precision.HIGHEST)
    return approx


def nothing(square):
    return jnp.zeros_like(square)


def shards(matrix):
    rows_dev, cols_dev = matrix.shape
    row_here = lax.axis_index("row")
    col_here = lax.axis_index("col")
    row_global = row_here * rows_dev + jnp.arange(rows_dev, dtype=jnp.int32)
    col_global = col_here * cols_dev + jnp.arange(cols_dev, dtype=jnp.int32)
    row_done = row_global < 0
    col_done = col_global < 0
    current = matrix
    owner_row = 0 // rows_dev
    owner_col = 0 // cols_dev
    row_offset = 0 - owner_row * rows_dev
    col_offset = 0 - owner_col * cols_dev
    row_done = row_done | (row_global >= 0) & (row_global < NB)
    col_done = col_done | (col_global >= 0) & (col_global < NB)
    upper_rows = current
    upper_wire = jnp.where(col_done[None, :], jnp.zeros_like(upper_rows), upper_rows).astype(
        jnp.bfloat16
    )
    corner = current[row_offset : row_offset + NB, col_offset : col_offset + NB]
    on_column = col_here == owner_col
    upper = broadcast(upper_wire, "row", owner_row)
    at_owner = on_column & (row_here == owner_row)
    local_inverse = lax.cond(at_owner, newton, nothing, corner)
    inverse = broadcast(local_inverse, "row", owner_row)
    pivot_columns = current[:, col_offset : col_offset + NB]
    done_now = row_done

    def multiply(operand):
        product = jnp.dot(pivot_columns, operand, precision=lax.Precision.HIGHEST)
        return jnp.where(done_now[:, None], jnp.zeros_like(product), product).astype(jnp.bfloat16)

    def skipped(operand):
        return jnp.zeros((rows_dev, NB), jnp.bfloat16)

    lower_local = lax.cond(on_column, multiply, skipped, inverse)
    lower = broadcast(lower_local, "col", owner_col)
    current = current - jnp.dot(lower, upper, preferred_element_type=jnp.float32)
    return current


def solution(mesh):
    return jax.shard_map(
        shards,
        mesh=mesh,
        in_specs=(P("row", "col"),),
        out_specs=P("row", "col"),
        check_vma=False,
    )
```

profile of v0, /device:TPU:16, one launch (start us, length us, event | category | flops | bytes accessed | tf_op | source)
XLA Modules:
  0.0 716.3 jit_solution(4387416971747851842)
XLA Ops:
  6.5 0.0 all-reduce.4.cloned.1.call-start
  6.5 1.0 slice.7
  7.6 0.0 copy-start
  7.6 0.7 broadcast_select_fusion
  8.3 0.0 all-reduce.4.cloned.1.call-update
  8.3 0.0 all-reduce.6.cloned.1.call-start
  8.4 290.2 %all-reduce.4.cloned.1.call-done = f32[256,256]{1,0:T(8,128)} async-done(((f32[256,256]{1,0:T(8,128)}), f32[256,256]{1,0:T(8,128)}) %all-reduce.4.cloned.1.call-update) | async-done | bytes 262160 | tf_op jit(solution)/shard_map/psum | solution.py:12
  298.6 0.7 broadcast_select_fusion.1
  299.3 0.0 all-reduce.6.cloned.1.call-update
  299.3 0.0 all-reduce.8.cloned.1.call-start
  299.3 0.0 copy-done
  299.4 0.9 fusion.6
  300.3 0.0 all-reduce.8.cloned.1.call-update
  300.3 118.4 %all-reduce.6.cloned.1.call-done = bf16[256,256]{1,0:T(8,128)(2,1)} async-done(((bf16[256,256]{1,0:T(8,128)(2,1)}), bf16[256,256]{1,0:T(8,128)(2,1)}) %all-reduce.6.cloned.1.call-update) | async-done | bytes 131088 | tf_op jit(solution)/shard_map/psum | solution.py:12
  418.7 288.6 %all-reduce.8.cloned.1.call-done = bf16[256,1024]{1,0:T(8,128)(2,1)} async-done(((bf16[256,1024]{1,0:T(8,128)(2,1)}), bf16[256,1024]{1,0:T(8,128)(2,1)}) %all-reduce.8.cloned.1.call-update) | async-done | bytes 524304 | tf_op jit(solution)/shard_map/psum | solution.py:12
  707.4 2.4 convolution_subtract_fusion
  (6 shorter events, 0.1 us)
Async XLA Ops:
  6.5 292.0 %all-reduce.4.cloned.1.call-start = ((), (), s32[]{:S(2)}) async-start(), calls=%async_computation | async-start | bytes 524288 | tf_op jit(solution)/shard_map/psum | solution.py:12
  7.6 291.8 %copy-start = (f32[256,1024]{1,0:T(8,128)S(1)}, f32[256,1024]{1,0:T(8,128)}, u32[]{:S(2)}) copy-start(f32[256,1024]{1,0:T(8,128)} %param.5) | copy-start | bytes 3145732
  8.3 410.4 %all-reduce.6.cloned.1.call-start = ((), (), s32[]{:S(2)}) async-start(), calls=%async_computation.1 | async-start | bytes 262144 | tf_op jit(solution)/shard_map/psum | solution.py:12
  299.3 408.1 %all-reduce.8.cloned.1.call-start = ((), (), s32[]{:S(2)}) async-start(), calls=%async_computation.2 | async-start | bytes 1048576 | tf_op jit(solution)/shard_map/psum | solution.py:12
Sparse Core Ops, SparseCore 0:
  10.8 287.7 all-reduce.3
  300.9 117.7 all-reduce.5
  422.2 285.1 all-reduce.7
where the time goes:
time: 717 us; the launch traced here: 716 us
  waiting for transfers between devices  697 us (97%)
  between operations  13.2 us (2%)
    psum x3, waiting for transfers between devices, broadcast(): return lax.psum(kept, axis)  697 us
  transfers between devices with their start and end apart: 3, of which 3 were waited for; matrix products, arithmetic and copies ran while one was open for 0% of the time, Pallas kernels for 0%

commit v1 on v0

v1 whole, which is shorter than its diff:
```python
import functools

import jax
import jax.numpy as jnp
from jax import lax
from jax.experimental import pallas as pl
from jax.experimental.pallas import tpu as pltpu
from jax.sharding import PartitionSpec as P

NB = 256
NX = 4
NZ = 16
NY = 8
CHUNKS = 4
MESH = pl.DeviceIdType.MESH
HIGH = lax.Precision.HIGHEST
F32 = jnp.float32
BF16 = jnp.bfloat16


def inverse_of(square):
    size = square.shape[0]
    eye = lax.broadcasted_iota(jnp.int32, (size, size), 0) == lax.broadcasted_iota(
        jnp.int32, (size, size), 1
    )
    diagonal = jnp.where(eye, square, 0.0)
    across = 1.0 / jnp.sum(diagonal, axis=0, keepdims=True)
    down = 1.0 / jnp.sum(diagonal, axis=1, keepdims=True)
    identity = jnp.where(eye, 1.0, 0.0)
    error = identity - square * across
    first = identity + error
    second = jnp.dot(error, error, precision=HIGH, preferred_element_type=F32)
    third = jnp.dot(first, second, precision=HIGH, preferred_element_type=F32)
    return down * (first + third)


def kernel(m_hbm, l_ref, u_ref, m_buf, x_buf, m_sem, send_sem, own_sem, ux_sem, xz_sem, xx_sem,
           ly_sem, ls_sem, z_ready, y_ready):
    row, col = lax.axis_index("row"), lax.axis_index("col")
    z, x = row // NX, row % NX
    y, core = col // 2, col % 2
    rows, cols = u_ref.shape
    quarter = rows // NX
    chunk = quarter // CHUNKS
    piece = NB // NX
    half = rows // 2
    at_root_row = row == 0
    at_first_col = col == 0
    at_root = at_root_row & at_first_col

    def at_x(j):
        return z * NX + (x + j) % NX

    def at_z(k):
        return ((z + k) % NZ) * NX + x

    def at_y(k, c):
        return ((y + k) % NY) * 2 + c

    load = pltpu.make_async_copy(m_hbm, m_buf, m_sem)
    load.start()
    barrier = pltpu.get_barrier_semaphore()
    near = [(at_x(1), col), (at_x(2), col), (at_x(3), col), (at_z(1), col), (at_z(NZ - 1), col),
            (row, at_y(1, core)), (row, at_y(NY - 1, core)), (row, at_y(0, 1 - core))]
    for device in near:
        pl.semaphore_signal(barrier, inc=1, device_id=device, device_id_type=MESH)

    sent = []

    def send(cond, src, dst, recv, device):
        copy = pltpu.make_async_remote_copy(
            src_ref=src, dst_ref=dst, send_sem=send_sem.at[len(sent)], recv_sem=recv,
            device_id=device, device_id_type=MESH,
        )
        sent.append((cond, copy))

        @pl.when(cond)
        def _():
            copy.start()

    def arrived(ref, sem):
        pltpu.make_async_copy(ref, ref, sem).wait()

    load.wait()

    @pl.when(at_root_row)
    def _():
        columns = col * cols + lax.broadcasted_iota(jnp.int32, (rows, cols), 1)
        u_ref[...] = jnp.where(columns < NB, 0.0, m_buf[...]).astype(BF16)

    @pl.when(at_root)
    def _():
        x_buf[...] = inverse_of(m_buf[:, 0:NB])

    pl.semaphore_wait(barrier, len(near))

    @pl.when(core == 0)
    def _():
        @pl.when((y != 0) & (y != NY // 2) & (y != NY // 2 + 1))
        def _():
            pl.semaphore_wait(y_ready, 1)

        @pl.when((y > 0) & (y <= NY // 2))
        def _():
            pl.semaphore_signal(y_ready, 1, device_id=(row, at_y(NY - 1, 0)), device_id_type=MESH)

        @pl.when(y > NY // 2)
        def _():
            pl.semaphore_signal(y_ready, 1, device_id=(row, at_y(1, 0)), device_id_type=MESH)

    @pl.when(at_first_col)
    def _():
        @pl.when((z != 0) & (z != NZ // 2) & (z != NZ // 2 + 1))
        def _():
            pl.semaphore_wait(z_ready, 1)

        @pl.when((z > 0) & (z <= NZ // 2))
        def _():
            pl.semaphore_signal(z_ready, 1, device_id=(at_z(NZ - 1), col), device_id_type=MESH)

        @pl.when(z > NZ // 2)
        def _():
            pl.semaphore_signal(z_ready, 1, device_id=(at_z(1), col), device_id_type=MESH)

    def x_part(q):
        return x_buf.at[pl.ds(pl.multiple_of(q * piece, piece), piece), :]

    def u_part(q, k):
        return u_ref.at[pl.ds(pl.multiple_of(q * quarter + k * chunk, chunk), chunk), :]

    def u_quarter(q):
        return u_ref.at[pl.ds(pl.multiple_of(q * quarter, quarter), quarter), :]

    for q in (2, 1, 3):
        send(at_root, x_part(q), x_part(q), xz_sem, (q, col))
    for k in range(CHUNKS):
        for q in (2, 1, 3):
            send(at_root_row, u_part(q, k), u_part(q, k), own_sem.at[k], (q, col))

    def spread_u(cond):
        for k in range(CHUNKS):
            @pl.when(cond & (row != 0))
            def _():
                arrived(u_part(x, k), own_sem.at[k])

            part = u_part(x, k)
            send(cond & (z < NZ // 2), part, part, own_sem.at[k], (at_z(1), col))
            send(cond & ((z == 0) | (z > NZ // 2 + 1)), part, part, own_sem.at[k], (at_z(NZ - 1), col))
            for j in (2, 1, 3):
                send(cond & (at_x(j) != 0), part, part, ux_sem.at[j - 1], (at_x(j), col))

    def spread_x(cond):
        @pl.when(cond & (row != 0))
        def _():
            arrived(x_part(x), xz_sem)

        @pl.when(cond & (z == 0))
        def _():
            pl.semaphore_wait(z_ready, 2)

        for k in (8, 7, 9, 6, 10, 5, 11, 4, 12, 3, 13, 2, 14, 1, 15):
            send(cond & (z == 0), x_part(x), x_part(x), xz_sem, (at_z(k), col))
        for j in (2, 1, 3):
            send(cond & (at_x(j) != 0), x_part(x), x_part(x), xx_sem.at[j - 1], (at_x(j), col))

    x_first = (z == 0) | ((z > 4) & (z < 12))
    spread_x(at_first_col & x_first)
    spread_u(row >= 0)
    spread_x(at_first_col & jnp.logical_not(x_first))

    @pl.when(at_first_col & (row != 0))
    def _():
        for j in (1, 2, 3):
            arrived(x_part((x + NX - j) % NX), xx_sem.at[j - 1])

    @pl.when(at_first_col)
    def _():
        pl.semaphore_wait(y_ready, 2)

    for h in (0, 1):
        part = l_ref.at[pl.ds(h * half, half), :]

        @pl.when(at_first_col)
        def _():
            product = jnp.dot(m_buf[pl.ds(h * half, half), 0:NB], x_buf[...], precision=HIGH,
                              preferred_element_type=F32)
            l_ref[pl.ds(h * half, half), :] = jnp.where(at_root_row, 0.0, product).astype(BF16)

        for k in (4, 3, 5, 2, 6, 1, 7):
            send(at_first_col, part, part, ly_sem, (row, at_y(k, h)))
        send(at_first_col, part, part, ly_sem if h == 1 else ls_sem, (row, 1))

    mine = l_ref.at[pl.ds(pl.multiple_of(core * half, half), half), :]
    other = l_ref.at[pl.ds(pl.multiple_of((1 - core) * half, half), half), :]

    @pl.when(col != 0)
    def _():
        arrived(mine, ly_sem)

    send(y != 0, mine, mine, ls_sem, (row, at_y(0, 1 - core)))

    @pl.when(col != 0)
    def _():
        arrived(other, ls_sem)

    @pl.when(row != 0)
    def _():
        for j in (1, 2, 3):
            arrived(u_quarter((x + NX - j) % NX), ux_sem.at[j - 1])

    for cond, copy in sent:
        @pl.when(cond)
        def _(copy=copy):
            copy.wait_send()


def shards(matrix):
    rows, cols = matrix.shape
    sends = 3 + 3 * CHUNKS + 5 * CHUNKS + 2 * 18 + 16 + 1
    lower, upper = pl.pallas_call(
        kernel,
        out_shape=(jax.ShapeDtypeStruct((rows, NB), BF16), jax.ShapeDtypeStruct((rows, cols), BF16)),
        in_specs=[pl.BlockSpec(memory_space=pl.ANY)],
        out_specs=(pl.BlockSpec(memory_space=pltpu.VMEM), pl.BlockSpec(memory_space=pltpu.VMEM)),
        scratch_shapes=[
            pltpu.VMEM((rows, cols), F32),
            pltpu.VMEM((NB, NB), F32),
            pltpu.SemaphoreType.DMA,
            pltpu.SemaphoreType.DMA((sends,)),
            pltpu.SemaphoreType.DMA((CHUNKS,)),
            pltpu.SemaphoreType.DMA((3,)),
            pltpu.SemaphoreType.DMA,
            pltpu.SemaphoreType.DMA((3,)),
            pltpu.SemaphoreType.DMA,
            pltpu.SemaphoreType.DMA,
            pltpu.SemaphoreType.REGULAR,
            pltpu.SemaphoreType.REGULAR,
        ],
        compiler_params=pltpu.CompilerParams(collective_id=0, has_side_effects=True),
    )(matrix)
    return matrix - jnp.dot(lower, upper, preferred_element_type=F32)


def solution(mesh):
    return jax.shard_map(
        shards,
        mesh=mesh,
        in_specs=(P("row", "col"),),
        out_specs=P("row", "col"),
        check_vma=False,
    )
```

time: 717 us -> 59.2 us (0.08)
  the two profiles are of different devices: /device:TPU:16 before, /device:TPU:265 now
where the time goes in v1:
time: 59.2 us; the launch traced here: 59 us
  Pallas kernels  56.6 us (96%)
  matrix products  2.39 us (4%)
    pallas_call x1, Pallas kernels, shards(): pl.pallas_call(kernel, out_shape=(jax.ShapeDtypeStruct((rows, NB), BF16),...  56.6 us
    dot_general x1, matrix products, shards(): return matrix - jnp.dot(lower, upper, preferred_element_type=F32)  2.39 us

profile of v1, /device:TPU:265, one launch (start us, length us, event | category | flops | bytes accessed | tf_op | source)
XLA Modules:
  0.0 59.0 jit_solution(17023160399963623402)
XLA Ops:
  0.0 0.0 copy-start
  0.0 56.6 %shard_map.17 = (bf16[256,256]{1,0:T(8,128)(2,1)}, bf16[256,1024]{1,0:T(8,128)(2,1)}) custom-call(f32[256,1024]{1,0:T(8,128)} %m_hbm.1), custom_call_target="tpu_custom_call" | custom-call | tf_op jit(solution)/shard_map/pallas_call | solution.py:220
  56.6 0.0 copy-done
  56.6 2.4 %convolution_subtract_fusion = f32[256,1024]{1,0:T(8,128)} fusion(f32[256,1024]{1,0:T(8,128)S(1)} %copy-done, bf16[256,256]{1,0:T(8,128)(2,1)} %get-tuple-element.7, bf16[256,1024]{1,0:T(8,128)(2,1)} %get-tuple-element.8), kind=kOutput, calls=%fused_computation | convolution fusion | flops 134479872 | bytes 2752512 | tf_op jit(solution)/shard_map/dot_general | solution.py:241
Async XLA Ops:
  0.0 56.6 %copy-start = (f32[256,1024]{1,0:T(8,128)S(1)}, f32[256,1024]{1,0:T(8,128)}, u32[]{:S(2)}) copy-start(f32[256,1024]{1,0:T(8,128)} %m_hbm.1) | copy-start | bytes 3145732

commit v2 on v1

v2 whole, which is shorter than its diff:
```python
import jax
import jax.numpy as jnp
from jax import lax
from jax.experimental import pallas as pl
from jax.experimental.pallas import tpu as pltpu
from jax.sharding import PartitionSpec as P

NB = 256
NX = 4
NZ = 16
NY = 8
CHUNKS = 4
MESH = pl.DeviceIdType.MESH
F32 = jnp.float32
BF16 = jnp.bfloat16


def split(a):
    high = a.astype(BF16)
    return high, (a - high.astype(F32)).astype(BF16)


def product(a, b):
    (ah, al), (bh, bl) = a, b
    dot = lambda u, v: jnp.dot(u, v, preferred_element_type=F32)
    return dot(ah, bh) + (dot(ah, bl) + dot(al, bh))


def inverse_of(square):
    size = square.shape[0]
    eye = lax.broadcasted_iota(jnp.int32, (size, size), 0) == lax.broadcasted_iota(
        jnp.int32, (size, size), 1
    )
    diagonal = jnp.where(eye, square, 0.0)
    across = 1.0 / jnp.sum(diagonal, axis=0, keepdims=True)
    down = 1.0 / jnp.sum(diagonal, axis=1, keepdims=True)
    identity = jnp.where(eye, 1.0, 0.0)
    error = identity - square * across
    first = identity + error
    parts = split(error)
    second = product(parts, parts)
    return down * (first + (second + product(parts, split(second))))


def kernel(m_ref, l_ref, u_ref, c_buf, parts, x_buf, send_sem, own_sem, ux_sem, mc_sem,
           xz_sem, xx_sem, ly_sem, ls_sem):
    row, col = lax.axis_index("row"), lax.axis_index("col")
    z, x = lax.div(row, NX), lax.rem(row, NX)
    y, core = lax.div(col, 2), lax.rem(col, 2)
    rows, cols = u_ref.shape
    quarter = rows // NX
    chunk = quarter // CHUNKS
    piece = NB // NX
    half = NB // 2
    top = row == 0
    plane = y == 0
    first_col = col == 0
    root = top & first_col

    plus = z <= NZ // 2
    away = jnp.where(plus, z, NZ - z)
    parent = jnp.where(
        plane, lax.div(jnp.maximum(away - 1, 0), 4) * 4, lax.div(jnp.maximum(away - 1, 0), 3) * 3
    )
    parent_z = jnp.where(plus, parent, lax.rem(NZ - parent, NZ))
    relay = jnp.where(plane, lax.rem(away, 4), lax.rem(away, 3)) == 0
    step = jnp.where(plane, 4, 3)

    def down_z(j):
        far = relay & (j <= step)
        return [
            (far & plus & (away + j <= NZ // 2), lax.rem(z + j, NZ)),
            (far & (jnp.logical_not(plus) | (z == 0)) & (away + j < NZ // 2), lax.rem(z + NZ - j, NZ)),
        ]

    children = sum(jnp.where(c, 1, 0) for j in (4, 3, 2, 1) for c, _ in down_z(j))

    def at_x(j):
        return z * NX + lax.rem(x + j, NX)

    barrier = pltpu.get_barrier_semaphore()

    def greet(device):
        pl.semaphore_signal(barrier, inc=1, device_id=device, device_id_type=MESH)

    for j in (1, 2, 3):
        greet((at_x(j), col))
    greet((row, y * 2 + 1 - core))

    @pl.when(z != 0)
    def _():
        greet((parent_z * NX + x, col))

    @pl.when((z == 0) & (x != 0) & (col == 1))
    def _():
        greet((0, 0))

    @pl.when(y != 0)
    def _():
        greet((row, core))

    sent = []

    def send(cond, src, dst, recv, device):
        copy = pltpu.make_async_remote_copy(
            src_ref=src, dst_ref=dst, send_sem=send_sem.at[len(sent)], recv_sem=recv,
            device_id=device, device_id_type=MESH,
        )
        sent.append((cond, copy))

        @pl.when(cond)
        def _():
            copy.start()

    def arrived(ref, sem):
        pltpu.make_async_copy(ref, ref, sem).wait()

    @pl.when(top)
    def _():
        columns = col * cols + lax.broadcasted_iota(jnp.int32, (rows, cols), 1)
        u_ref[...] = jnp.where(columns < NB, 0.0, m_ref[...]).astype(BF16)

    @pl.when(root)
    def _():
        inverse = inverse_of(m_ref[:, :NB])
        x_buf[0] = inverse[:, :half]
        x_buf[1] = inverse[:, half:]

    pl.semaphore_wait(
        barrier, 4 + children + jnp.where(plane, NY - 1, 0) + jnp.where(root, NX - 1, 0)
    )

    def x_part(h, q):
        return x_buf.at[h, pl.ds(pl.multiple_of(q * piece, piece), piece), :]

    def u_part(q, k):
        return u_ref.at[pl.ds(pl.multiple_of(q * quarter + k * chunk, chunk), chunk), :]

    def u_quarter(q):
        return u_ref.at[pl.ds(pl.multiple_of(q * quarter, quarter), quarter), :]

    send(root, x_part(1, 0), x_part(1, 0), xz_sem, (0, 1))
    for q in (2, 1, 3):
        for h in (1, 0):
            send(root, x_part(h, q), x_part(h, q), xz_sem, (q, h))
    for k in range(CHUNKS):
        for q in (2, 1, 3):
            send(top, u_part(q, k), u_part(q, k), own_sem.at[k], (q, col))
    send(first_col, m_ref.at[:, pl.ds(0, NB)], c_buf, mc_sem, (row, 1))

    @pl.when(plane & jnp.logical_not(root))
    def _():
        arrived(x_part(core, x), xz_sem)

    mine = x_part(core, x)
    for j in (4, 3, 2, 1):
        for cond, to in down_z(j):
            send(plane & cond, mine, mine, xz_sem, (to * NX + x, col))
    for j in (2, 1, 3):
        send(plane & (at_x(j) != 0), mine, mine, xx_sem.at[j - 1], (at_x(j), col))

    def spread(cond, down):
        for k in range(CHUNKS):
            part = u_part(x, k)

            @pl.when(cond & jnp.logical_not(top))
            def _():
                arrived(part, own_sem.at[k])

            if down:
                for j in (4, 3, 2, 1):
                    for further, to in down_z(j):
                        send(cond & further, part, part, own_sem.at[k], (to * NX + x, col))
            for j in (2, 1, 3):
                send(cond & (at_x(j) != 0), part, part, ux_sem.at[j - 1], (at_x(j), col))

    spread(relay, True)

    @pl.when(first_col)
    def _():
        parts[0], parts[1] = split(m_ref[:, :NB])

    @pl.when(col == 1)
    def _():
        arrived(c_buf, mc_sem)
        parts[0], parts[1] = split(c_buf[...])

    own = pl.ds(pl.multiple_of(core * half, half), half)
    other = pl.ds(pl.multiple_of((1 - core) * half, half), half)

    @pl.when(plane & jnp.logical_not(top))
    def _():
        for j in (1, 2, 3):
            arrived(x_part(core, lax.rem(x + NX - j, NX)), xx_sem.at[j - 1])
        l_ref[:, own] = product((parts[0], parts[1]), split(x_buf[core])).astype(BF16)

    @pl.when(plane & top)
    def _():
        l_ref[:, own] = jnp.zeros((rows, half), BF16)

    for k in (4, 3, 5, 2, 6, 1, 7):
        send(plane, l_ref.at[:, own], l_ref.at[:, own], ly_sem, (row, k * 2 + core))

    spread(jnp.logical_not(relay), False)

    @pl.when(jnp.logical_not(plane))
    def _():
        arrived(l_ref.at[:, own], ly_sem)

    send(row >= 0, l_ref.at[:, own], l_ref.at[:, own], ls_sem, (row, y * 2 + 1 - core))

    @pl.when(row != 0)
    def _():
        for j in (1, 2, 3):
            arrived(u_quarter(lax.rem(x + NX - j, NX)), ux_sem.at[j - 1])

    arrived(l_ref.at[:, other], ls_sem)

    @pl.when(plane & top & (x != 0))
    def _():
        for j in (1, 2, 3):
            arrived(x_part(core, lax.rem(x + NX - j, NX)), xx_sem.at[j - 1])

    for cond, copy in sent:
        @pl.when(cond)
        def _(copy=copy):
            copy.wait_send()


def shards(matrix):
    rows, cols = matrix.shape
    lower, upper = pl.pallas_call(
        kernel,
        out_shape=(jax.ShapeDtypeStruct((rows, NB), BF16), jax.ShapeDtypeStruct((rows, cols), BF16)),
        in_specs=[pl.BlockSpec(memory_space=pltpu.VMEM)],
        out_specs=(pl.BlockSpec(memory_space=pltpu.VMEM), pl.BlockSpec(memory_space=pltpu.VMEM)),
        scratch_shapes=[
            pltpu.VMEM((rows, NB), F32),
            pltpu.VMEM((2, rows, NB), BF16),
            pltpu.VMEM((2, NB, NB // 2), F32),
            pltpu.SemaphoreType.DMA((128,)),
            pltpu.SemaphoreType.DMA((CHUNKS,)),
            pltpu.SemaphoreType.DMA((3,)),
            pltpu.SemaphoreType.DMA,
            pltpu.SemaphoreType.DMA,
            pltpu.SemaphoreType.DMA((3,)),
            pltpu.SemaphoreType.DMA,
            pltpu.SemaphoreType.DMA,
        ],
        compiler_params=pltpu.CompilerParams(
            collective_id=0, has_side_effects=True, vmem_limit_bytes=24 * 1024 * 1024
        ),
    )(matrix)
    return matrix - jnp.dot(lower, upper, preferred_element_type=F32)


def solution(mesh):
    return jax.shard_map(
        shards,
        mesh=mesh,
        in_specs=(P("row", "col"),),
        out_specs=P("row", "col"),
        check_vma=False,
    )
```

time: 59.2 us -> 43.4 us (0.73)
  the two profiles are of different devices: /device:TPU:265 before, /device:TPU:64 now
where the time goes in v2:
time: 43.4 us; the launch traced here: 43.2 us
  Pallas kernels  40.7 us (94%)
  matrix products  1.28 us (3%)
  local copies, waits for them, and re-layouts  1.22 us (3%)
    pallas_call x1, Pallas kernels, shards(): pl.pallas_call(kernel, out_shape=(jax.ShapeDtypeStruct((rows, NB), BF16),...  40.7 us
    dot_general x1, matrix products, shards(): return matrix - jnp.dot(lower, upper, preferred_element_type=F32)  1.28 us
    unnamed x2, local copies, waits for them, and re-layouts  1.22 us

profile of v2, /device:TPU:64, one launch (start us, length us, event | category | flops | bytes accessed | tf_op | source)
XLA Modules:
  0.0 43.2 jit_solution(1649390427837225903)
XLA Ops:
  0.0 0.0 copy-start
  0.0 1.2 %copy-done = f32[256,1024]{1,0:T(8,128)S(1)} copy-done((f32[256,1024]{1,0:T(8,128)S(1)}, f32[256,1024]{1,0:T(8,128)}, u32[]{:S(2)}) %copy-start) | copy-done | bytes 1048600
  1.2 40.7 %shard_map.17 = (bf16[256,256]{1,0:T(8,128)(2,1)S(1)}, bf16[256,1024]{1,0:T(8,128)(2,1)S(1)}) custom-call(f32[256,1024]{1,0:T(8,128)S(1)} %copy-done), custom_call_target="tpu_custom_call" | custom-call | tf_op jit(solution)/shard_map/pallas_call | solution.py:232
  41.9 1.3 %convolution_subtract_fusion = f32[256,1024]{1,0:T(8,128)} fusion(f32[256,1024]{1,0:T(8,128)S(1)} %copy-done, bf16[256,256]{1,0:T(8,128)(2,1)S(1)} %get-tuple-element.7, bf16[256,1024]{1,0:T(8,128)(2,1)S(1)} %get-tuple-element.8), kind=kOutput, calls=%fused_computation | convolution fusion | flops 134479872 | bytes 2752512 | tf_op jit(solution)/shard_map/dot_general | solution.py:254
Async XLA Ops:
  0.0 1.2 %copy-start = (f32[256,1024]{1,0:T(8,128)S(1)}, f32[256,1024]{1,0:T(8,128)}, u32[]{:S(2)}) copy-start(f32[256,1024]{1,0:T(8,128)} %m_ref.1) | copy-start | bytes 3145732

commit v3 on v2

v3 whole, which is shorter than its diff:
```python
import jax
import jax.numpy as jnp
from jax import lax
from jax.experimental import pallas as pl
from jax.experimental.pallas import tpu as pltpu
from jax.sharding import PartitionSpec as P

NB = 256
NX = 4
NZ = 16
NY = 8
CHAIN = 8
HUB = 13
CHUNKS = 4
MESH = pl.DeviceIdType.MESH
F32 = jnp.float32
BF16 = jnp.bfloat16


def split(a):
    high = a.astype(BF16)
    return high, (a - high.astype(F32)).astype(BF16)


def product(a, b):
    (ah, al), (bh, bl) = a, b
    dot = lambda u, v: jnp.dot(u, v, preferred_element_type=F32)
    return dot(ah, bh) + (dot(ah, bl) + dot(al, bh))


def inverse_of(square):
    size = square.shape[0]
    eye = lax.broadcasted_iota(jnp.int32, (size, size), 0) == lax.broadcasted_iota(
        jnp.int32, (size, size), 1
    )
    diagonal = jnp.where(eye, square, 0.0)
    across = 1.0 / jnp.sum(diagonal, axis=0, keepdims=True)
    down = 1.0 / jnp.sum(diagonal, axis=1, keepdims=True)
    identity = jnp.where(eye, 1.0, 0.0)
    error = identity - square * across
    first = identity + error
    parts = split(error)
    second = product(parts, parts)
    return down * (first + (second + product(parts, split(second))))


def kernel(m_ref, l_ref, u_ref, x_buf, send_sem, own_sem, ux_sem, xz_sem, xx_sem, ly_sem, ls_sem,
           ready_x, ready_y, ready_z, ready_w, ready_v):
    row, col = lax.axis_index("row"), lax.axis_index("col")
    z, x = lax.div(row, NX), lax.rem(row, NX)
    y, core = lax.div(col, 2), lax.rem(col, 2)
    rows, cols = u_ref.shape
    quarter = rows // NX
    chunk = quarter // CHUNKS
    piece = NB // NX
    half = NB // 2
    top = row == 0
    below = row != 0
    first_col = col == 0
    other_col = col != 0
    root = top & first_col
    bottom = z == 0
    one = lambda cond: jnp.where(cond, 1, 0)

    hub = z == HUB
    chain = (z < CHAIN) & (lax.rem(z, 2) == 0)
    beyond = [(hub, HUB + j) for j in (-1, 1, -2, 2, -3, -4)]
    down_u = [(chain, z + 2), (chain, z + 1)] + beyond
    step = first_col & ((z == 0) | (z == 4))
    down_x = [(step, z + j) for j in (1, 2, 3, 4)] + [(first_col & hub, to) for _, to in beyond]
    extra = [(step, z + 3), (step, z + 4)]
    parent_z = jnp.where(z > CHAIN, HUB, jnp.where(lax.rem(z, 2) == 0, z - 2, z - 1))
    second_parent = first_col & ((z == 3) | (z == 4) | (z == 7) | (z == 8))
    second_z = jnp.where(z < 5, 0, 4)

    def at_x(j):
        return z * NX + lax.rem(x + j, NX)

    from_root_x = bottom & (x != 0) & first_col
    from_root_z = (z > 0) & (z < 5) & (x == 0) & first_col
    by_parent = (z > 2) | ((z > 0) & jnp.logical_not(from_root_z))
    by_second = second_parent & jnp.logical_not(from_root_z)

    barrier = pltpu.get_barrier_semaphore()

    def signal(cond, sem, device):
        @pl.when(cond)
        def _():
            pl.semaphore_signal(sem, inc=1, device_id=device, device_id_type=MESH)

    usual = jnp.logical_not(root)
    signal(from_root_x | from_root_z, barrier, (0, 0))
    signal(row >= 0, barrier, (row, y * 2 + 1 - core))
    for j in (1, 2, 3):
        signal(usual & (x + j < NX), barrier, (row + j, col))
    for cond, to in down_u + extra:
        signal(usual & cond, barrier, (to * NX + x, col))
    signal(bottom, barrier, (HUB * NX + x, col))
    for k in range(2, 2 * NY):
        signal(below & first_col, barrier, (row, k))
    signal(below & (y == 2), barrier, (row, 8 + core))

    pl.semaphore_wait(
        barrier,
        jnp.where(root, 1 + NX - 1 + 4,
                  1 + x - one(from_root_x) + one(by_parent) + one(by_second)
                  + one(below & (y != 0)) + one(below & (y == 4))),
    )

    for j in (1, 2, 3):
        signal((x >= j) & jnp.logical_not(from_root_x & (x == j)), ready_x, (row - j, col))
    signal(by_parent & jnp.logical_not(hub), ready_z, (parent_z * NX + x, col))
    signal(by_second, ready_z, (second_z * NX + x, col))
    signal(hub, ready_w, (x, col))
    signal(below & (y != 0), ready_y, (row, 0))
    signal(below & (y == 4), ready_v, (row, 4 + core))

    sent = []

    def send(cond, part, recv, device):
        copy = pltpu.make_async_remote_copy(
            src_ref=part, dst_ref=part, send_sem=send_sem.at[len(sent)], recv_sem=recv,
            device_id=device, device_id_type=MESH,
        )
        sent.append((cond, copy))

        @pl.when(cond)
        def _():
            copy.start()

    def arrived(ref, sem):
        pltpu.make_async_copy(ref, ref, sem).wait()

    def wait_for(cond, sem, count):
        @pl.when(cond)
        def _():
            pl.semaphore_wait(sem, count)

    def x_part(q):
        return x_buf.at[pl.ds(pl.multiple_of(q * piece, piece), piece), :]

    def u_part(q, k, first):
        return u_ref.at[
            pl.ds(pl.multiple_of(q * quarter + k * chunk, chunk), chunk), pl.ds(first, cols - first)
        ]

    def u_quarter(q, first):
        return u_ref.at[pl.ds(pl.multiple_of(q * quarter, quarter), quarter), pl.ds(first, cols - first)]

    def scatter_u(cond, first):
        for k in range(CHUNKS):
            for q in (2, 1, 3):
                send(cond, u_part(q, k, first), own_sem.at[k], (q, col))

    def spread_u(cond, first):
        for k in range(CHUNKS):
            part = u_part(x, k, first)

            @pl.when(cond & below)
            def _():
                arrived(part, own_sem.at[k])

            for j in (2, 1, 3):
                send(cond & (at_x(j) != 0), part, ux_sem.at[j - 1], (at_x(j), col))
            for further, to in down_u:
                send(cond & further, part, own_sem.at[k], (to * NX + x, col))

    def late_u(cond, first):
        for k in range(CHUNKS):
            send(cond & bottom, u_part(x, k, first), own_sem.at[k], (HUB * NX + x, col))

    @pl.when(root)
    def _():
        x_buf[...] = inverse_of(m_ref[:, :NB])

    for q in (2, 1, 3):
        send(root, x_part(q), xz_sem, (q, 0))

    @pl.when(top)
    def _():
        columns = col * cols + lax.broadcasted_iota(jnp.int32, (rows, cols), 1)
        u_ref[...] = jnp.where(columns < NB, 0.0, m_ref[...]).astype(BF16)
        l_ref[...] = jnp.zeros((rows, NB), BF16)

    @pl.when(first_col & below)
    def _():
        u_ref[:, :NB] = jnp.zeros((rows, NB), BF16)

    wait_for(usual & (x != NX - 1), ready_x, NX - 1 - x)
    scatter_u(top & other_col, 0)
    wait_for(usual & (chain | hub), ready_z, jnp.where(hub, 6, jnp.where(step, 4, 2)))
    spread_u(other_col, 0)
    wait_for(bottom & other_col, ready_w, 1)
    late_u(other_col, 0)

    @pl.when(first_col & below)
    def _():
        arrived(x_part(x), xz_sem)

    mine = x_part(x)
    for j in (2, 1, 3):
        send(first_col & (at_x(j) != 0), mine, xx_sem.at[j - 1], (at_x(j), 0))
    for cond, to in down_x:
        send(cond, mine, xz_sem, (to * NX + x, 0))
    scatter_u(root, NB)
    wait_for(bottom & first_col, ready_w, 1)
    send(bottom & first_col, mine, xz_sem, (HUB * NX + x, 0))

    @pl.when(first_col & below)
    def _():
        left = split(m_ref[:, :NB])
        for j in (1, 2, 3):
            arrived(x_part(lax.rem(x + NX - j, NX)), xx_sem.at[j - 1])
        l_ref[...] = product(left, split(x_buf[...])).astype(BF16)
        pl.semaphore_wait(ready_y, 2 * NY - 2)

    def l_part(h):
        return l_ref.at[pl.ds(pl.multiple_of(h * half, half), half), :]

    for k in (2, 6, 3, 7, 1, 5):
        for h in (0, 1):
            send(first_col & below, l_part(h), ly_sem, (row, k * 2 + h))
    send(first_col & below, l_ref, ly_sem, (row, 1))

    spread_u(first_col, NB)
    late_u(first_col, NB)

    @pl.when(below & (y != 0))
    def _():
        arrived(l_part(core), ly_sem)

    wait_for(below & (y == 2), ready_v, 1)
    send(below & (y == 2), l_part(core), ly_sem, (row, 8 + core))
    send(below & (y != 0), l_part(core), ls_sem, (row, y * 2 + 1 - core))

    for cond, first in ((other_col, 0), (first_col, NB)):
        @pl.when(cond & below)
        def _():
            for j in (1, 2, 3):
                arrived(u_quarter(lax.rem(x + NX - j, NX), first), ux_sem.at[j - 1])

    @pl.when(below & (y != 0))
    def _():
        arrived(l_part(1 - core), ls_sem)

    @pl.when(below & (col == 1))
    def _():
        arrived(l_ref, ly_sem)

    for cond, copy in sent:
        @pl.when(cond)
        def _(copy=copy):
            copy.wait_send()


def shards(matrix):
    rows, cols = matrix.shape
    lower, upper = pl.pallas_call(
        kernel,
        out_shape=(jax.ShapeDtypeStruct((rows, NB), BF16), jax.ShapeDtypeStruct((rows, cols), BF16)),
        in_specs=[pl.BlockSpec(memory_space=pltpu.VMEM)],
        out_specs=(pl.BlockSpec(memory_space=pltpu.VMEM), pl.BlockSpec(memory_space=pltpu.VMEM)),
        scratch_shapes=[
            pltpu.VMEM((NB, NB), F32),
            pltpu.SemaphoreType.DMA((160,)),
            pltpu.SemaphoreType.DMA((CHUNKS,)),
            pltpu.SemaphoreType.DMA((3,)),
            pltpu.SemaphoreType.DMA,
            pltpu.SemaphoreType.DMA((3,)),
            pltpu.SemaphoreType.DMA,
            pltpu.SemaphoreType.DMA,
        ]
        + [pltpu.SemaphoreType.REGULAR] * 5,
        compiler_params=pltpu.CompilerParams(
            collective_id=0, has_side_effects=True, vmem_limit_bytes=24 * 1024 * 1024
        ),
    )(matrix)
    return matrix - jnp.dot(lower, upper, preferred_element_type=F32)


def solution(mesh):
    return jax.shard_map(
        shards,
        mesh=mesh,
        in_specs=(P("row", "col"),),
        out_specs=P("row", "col"),
        check_vma=False,
    )
```

time: 43.4 us -> 39.9 us (0.919)
  the two profiles are of different devices: /device:TPU:64 before, /device:TPU:481 now
where the time goes in v3:
time: 39.9 us; the launch traced here: 39.7 us
  Pallas kernels  37.2 us (93%)
  matrix products  1.28 us (3%)
  local copies, waits for them, and re-layouts  1.22 us (3%)
    pallas_call x1, Pallas kernels, shards(): pl.pallas_call(kernel, out_shape=(jax.ShapeDtypeStruct((rows, NB), BF16),...  37.2 us
    dot_general x1, matrix products, shards(): return matrix - jnp.dot(lower, upper, preferred_element_type=F32)  1.28 us
    unnamed x2, local copies, waits for them, and re-layouts  1.22 us

profile of v3, /device:TPU:481, one launch (start us, length us, event | category | flops | bytes accessed | tf_op | source)
XLA Modules:
  0.0 39.7 jit_solution(3206447866600394918)
XLA Ops:
  0.0 0.0 copy-start
  0.0 1.2 %copy-done = f32[256,1024]{1,0:T(8,128)S(1)} copy-done((f32[256,1024]{1,0:T(8,128)S(1)}, f32[256,1024]{1,0:T(8,128)}, u32[]{:S(2)}) %copy-start) | copy-done | bytes 1048600
  1.2 37.2 %shard_map.17 = (bf16[256,256]{1,0:T(8,128)(2,1)S(1)}, bf16[256,1024]{1,0:T(8,128)(2,1)S(1)}) custom-call(f32[256,1024]{1,0:T(8,128)S(1)} %copy-done), custom_call_target="tpu_custom_call" | custom-call | tf_op jit(solution)/shard_map/pallas_call | solution.py:258
  38.4 1.3 %convolution_subtract_fusion = f32[256,1024]{1,0:T(8,128)} fusion(f32[256,1024]{1,0:T(8,128)S(1)} %copy-done, bf16[256,256]{1,0:T(8,128)(2,1)S(1)} %get-tuple-element.7, bf16[256,1024]{1,0:T(8,128)(2,1)S(1)} %get-tuple-element.8), kind=kOutput, calls=%fused_computation | convolution fusion | flops 134479872 | bytes 2752512 | tf_op jit(solution)/shard_map/dot_general | solution.py:278
Async XLA Ops:
  0.0 1.2 %copy-start = (f32[256,1024]{1,0:T(8,128)S(1)}, f32[256,1024]{1,0:T(8,128)}, u32[]{:S(2)}) copy-start(f32[256,1024]{1,0:T(8,128)} %m_ref.1) | copy-start | bytes 3145732

commit v4 on v3

v4 whole, which is shorter than its diff:
```python
import jax
import jax.numpy as jnp
from jax import lax
from jax.experimental import pallas as pl
from jax.experimental.pallas import tpu as pltpu
from jax.sharding import PartitionSpec as P

NB = 256
NX = 4
NZ = 16
NY = 8
CHAIN = 8
HUB = 13
NEAR = 6
CHUNKS = 4
MESH = pl.DeviceIdType.MESH
F32 = jnp.float32
BF16 = jnp.bfloat16


def split(a):
    high = a.astype(BF16)
    return high, (a - high.astype(F32)).astype(BF16)


def product(a, b):
    (ah, al), (bh, bl) = a, b
    dot = lambda u, v: jnp.dot(u, v, preferred_element_type=F32)
    return dot(ah, bh) + (dot(ah, bl) + dot(al, bh))


def inverse_of(square):
    size = square.shape[0]
    eye = lax.broadcasted_iota(jnp.int32, (size, size), 0) == lax.broadcasted_iota(
        jnp.int32, (size, size), 1
    )
    diagonal = jnp.where(eye, square, 0.0)
    across = 1.0 / jnp.sum(diagonal, axis=0, keepdims=True)
    down = 1.0 / jnp.sum(diagonal, axis=1, keepdims=True)
    identity = jnp.where(eye, 1.0, 0.0)
    error = identity - square * across
    first = identity + error
    parts = split(error)
    second = product(parts, parts)
    return down * (first + (second + product(parts, split(second))))


def kernel(m_hbm, l_ref, u_ref, m_ref, x_buf, m_sem, send_sem, own_sem, ux_sem, xz_sem, xx_sem, ly_sem, ls_sem,
           ready_x, ready_y, ready_z, ready_w, ready_v):
    row, col = lax.axis_index("row"), lax.axis_index("col")
    z, x = lax.div(row, NX), lax.rem(row, NX)
    y, core = lax.div(col, 2), lax.rem(col, 2)
    rows, cols = u_ref.shape
    quarter = rows // NX
    chunk = quarter // CHUNKS
    piece = NB // NX
    half = NB // 2
    top = row == 0
    below = row != 0
    first_col = col == 0
    other_col = col != 0
    root = top & first_col
    bottom = z == 0
    one = lambda cond: jnp.where(cond, 1, 0)

    hub = z == HUB
    chain = other_col & (z <= CHAIN) & (lax.rem(z, 2) == 0)
    source = first_col & bottom
    relay = first_col & (z == 4)
    first_hub = first_col & hub
    other_hub = other_col & hub
    down_u = [(chain, z + 2), (chain, z + 1)] + [(other_hub, to) for to in (12, 14, 11, 15)]
    down_x = (
        [(source, to) for to in range(1, NEAR + 1)] + [(relay, 7), (relay, 8)]
        + [(first_hub, to) for to in (9, 14, 10, 15, 11, 12)]
    )
    parent_z = jnp.where(
        first_col,
        jnp.where(z <= NEAR, 0, jnp.where(z < 9, 4, HUB)),
        jnp.where(z > CHAIN + 2, HUB, jnp.where(lax.rem(z, 2) == 0, z - 2, z - 1)),
    )
    children = (jnp.where(source, NEAR, 0) + jnp.where(relay, 2, 0) + jnp.where(first_hub, 6, 0)
                + jnp.where(chain, 2, 0) + jnp.where(other_hub, 4, 0))

    def at_x(j):
        return z * NX + lax.rem(x + j, NX)

    from_root_x = bottom & (x != 0) & first_col
    from_root_z = (z > 0) & (z <= NEAR) & (x == 0) & first_col
    by_parent = (z > 0) & jnp.logical_not(from_root_z)

    narrow = pltpu.make_async_copy(m_hbm.at[:, pl.ds(0, NB)], m_ref.at[:, pl.ds(0, NB)], m_sem.at[0])
    rest = pl.ds(NB, cols - NB)
    wide = pltpu.make_async_copy(m_hbm.at[:, rest], m_ref.at[:, rest], m_sem.at[1])

    @pl.when(first_col | top)
    def _():
        narrow.start()

    @pl.when(top)
    def _():
        wide.start()

    barrier = pltpu.get_barrier_semaphore()

    usual = jnp.logical_not(root)

    def signal(cond, sem, device):
        one_more = lambda: pl.semaphore_signal(sem, inc=1, device_id=device, device_id_type=MESH)
        one_more() if cond is None else pl.when(cond)(one_more)

    paired = below | (y != 0)
    signal(paired, barrier, (row, y * 2 + 1 - core))
    signal((row == 1) & (col == 1), barrier, (0, 1))
    signal(bottom, barrier, (HUB * NX + x, col))

    @pl.when(usual)
    def _():
        signal(from_root_x | from_root_z, barrier, (0, 0))
        for j in (1, 2, 3):
            signal(x + j < NX, barrier, (row + j, col))
        for cond, to in down_u + down_x:
            signal(cond, barrier, (to * NX + x, col))

    @pl.when(below & first_col)
    def _():
        for k in range(2, 2 * NY):
            signal(None, barrier, (row, k))

    signal(below & (y == 2), barrier, (row, 8 + core))

    pl.semaphore_wait(
        barrier,
        jnp.where(root, NX - 1 + NEAR,
                  one(paired) + one(top & (col == 1)) + x - one(from_root_x) + one(by_parent)
                  + one(below & (y != 0)) + one(below & (y == 4))),
    )

    @pl.when(usual)
    def _():
        for j in (1, 2, 3):
            signal((x >= j) & jnp.logical_not(from_root_x & (x == j)), ready_x, (row - j, col))
        signal(by_parent & jnp.logical_not(hub), ready_z, (parent_z * NX + x, col))
        signal(hub, ready_w, (x, col))
        signal(below & (y != 0), ready_y, (row, 0))
        signal(below & (y == 4), ready_v, (row, 4 + core))

    sections = []
    used = [0]

    def section(cond, body):
        group = []

        def send(part, recv, device, only=None):
            spot = used[0]
            used[0] += 1

            def begin():
                ref = part()
                pltpu.make_async_remote_copy(
                    src_ref=ref, dst_ref=ref, send_sem=send_sem.at[spot], recv_sem=recv,
                    device_id=device, device_id_type=MESH,
                ).start()

            group.append((only, part, spot))
            begin() if only is None else pl.when(only)(begin)

        pl.when(cond)(lambda: body(send))
        sections.append((cond, group))

    def arrived(ref, sem):
        pltpu.make_async_copy(ref, ref, sem).wait()

    def wait_for(cond, sem, count):
        @pl.when(cond)
        def _():
            pl.semaphore_wait(sem, count)

    def x_part(q):
        return x_buf.at[pl.ds(pl.multiple_of(q * piece, piece), piece), :]

    def u_part(q, k, first):
        return u_ref.at[
            pl.ds(pl.multiple_of(q * quarter + k * chunk, chunk), chunk), pl.ds(first, cols - first)
        ]

    def u_quarter(q, first):
        return u_ref.at[pl.ds(pl.multiple_of(q * quarter, quarter), quarter), pl.ds(first, cols - first)]

    def first_part(q, k):
        rows_here = pl.ds(pl.multiple_of(q * quarter + k * (quarter // 2), quarter // 2), quarter // 2)
        return u_ref.at[rows_here, pl.ds(NB, cols - NB)]

    def scatter_u(first):
        def body(send):
            for k in range(CHUNKS):
                for q in (2, 1, 3):
                    send(lambda q=q, k=k: u_part(q, k, first), own_sem.at[k], (q, col))
        return body

    not_back = [at_x(j) != 0 for j in (1, 2, 3)]

    def spread_u(first):
        def body(send):
            for k in range(CHUNKS):
                part = lambda k=k: u_part(x, k, first)

                @pl.when(below)
                def _():
                    arrived(part(), own_sem.at[k])

                for j in (2, 1, 3):
                    send(part, ux_sem.at[j - 1], (at_x(j), col), not_back[j - 1])
                for further, to in down_u:
                    send(part, own_sem.at[k], (to * NX + x, col), further)
        return body

    def late_u(first):
        def body(send):
            for k in range(CHUNKS):
                send(lambda k=k: u_part(x, k, first), own_sem.at[k], (HUB * NX + x, col))
        return body

    @pl.when(first_col | top)
    def _():
        narrow.wait()

    def start(send):
        x_buf[...] = inverse_of(m_ref[:, :NB])
        for q in (2, 1, 3):
            send(lambda q=q: x_part(q), xz_sem, (q, 0))

    section(root, start)

    @pl.when(top)
    def _():
        wide.wait()
        columns = col * cols + lax.broadcasted_iota(jnp.int32, (rows, cols), 1)
        u_ref[...] = jnp.where(columns < NB, 0.0, m_ref[...]).astype(BF16)
        l_ref[...] = jnp.zeros((rows, NB), BF16)

    wait_for(usual & (x != NX - 1), ready_x, NX - 1 - x)
    wait_for(usual & (children > 0), ready_z, children)

    section(top & other_col, scatter_u(0))
    section(other_col, spread_u(0))

    def last(first):
        def body(send):
            pl.semaphore_wait(ready_w, 1)
            late_u(first)(send)
        return body

    section(bottom & other_col, last(0))

    def inverse_rows(send):
        @pl.when(below)
        def _():
            u_ref[:, :NB] = jnp.zeros((rows, NB), BF16)
            arrived(x_part(x), xz_sem)

        mine = lambda: x_part(x)
        for j in (2, 1, 3):
            send(mine, xx_sem.at[j - 1], (at_x(j), 0), not_back[j - 1])
        for cond, to in down_x:
            send(mine, xz_sem, (to * NX + x, 0), cond)

    section(first_col, inverse_rows)

    def scatter_first(send):
        for k in range(2):
            for q in (2, 1, 3):
                send(lambda q=q, k=k: first_part(q, k), own_sem.at[k], (q, col))

    section(root, scatter_first)

    def to_hub(send):
        pl.semaphore_wait(ready_w, 1)
        send(lambda: x_part(x), xz_sem, (HUB * NX + x, 0))

    section(first_col & bottom, to_hub)

    def l_part(h):
        return l_ref.at[pl.ds(pl.multiple_of(h * half, half), half), :]

    def make_lower(send):
        left = split(m_ref[:, :NB])
        for j in (1, 2, 3):
            arrived(x_part(lax.rem(x + NX - j, NX)), xx_sem.at[j - 1])
        l_ref[...] = product(left, split(x_buf[...])).astype(BF16)
        pl.semaphore_wait(ready_y, 2 * NY - 2)
        for k in (2, 6, 3, 7, 1, 5):
            for h in (0, 1):
                send(lambda h=h: l_part(h), ly_sem, (row, k * 2 + h))
        send(lambda: l_ref, ly_sem, (row, 1))

    section(first_col & below, make_lower)

    def spread_first(send):
        for k in range(2):
            @pl.when(below)
            def _():
                arrived(first_part(x, k), own_sem.at[k])

            for j in (2, 1, 3):
                send(lambda k=k: first_part(x, k), ux_sem.at[j - 1], (at_x(j), col), not_back[j - 1])
        for cond, to in down_x + [(bottom, HUB)]:
            for k in range(2):
                send(lambda k=k: first_part(x, k), own_sem.at[k], (to * NX + x, col), cond)

    section(first_col, spread_first)

    passes = y == 2

    def relay_lower(send):
        arrived(l_part(core), ly_sem)

        @pl.when(passes)
        def _():
            pl.semaphore_wait(ready_v, 1)

        send(lambda: l_part(core), ly_sem, (row, 8 + core), passes)
        send(lambda: l_part(core), ls_sem, (row, y * 2 + 1 - core))

    section(below & (y != 0), relay_lower)

    def finish(first):
        for j in (1, 2, 3):
            arrived(u_quarter(lax.rem(x + NX - j, NX), first), ux_sem.at[j - 1])

    pl.when(below & other_col)(lambda: finish(0))
    pl.when(below & first_col)(lambda: finish(NB))

    @pl.when(below & (y != 0))
    def _():
        arrived(l_part(1 - core), ls_sem)

    @pl.when(below & (col == 1))
    def _():
        arrived(l_ref, ly_sem)

    def sent(group):
        for only, part, spot in group:
            gone = lambda part=part, spot=spot: arrived(part(), send_sem.at[spot])
            gone() if only is None else pl.when(only)(gone)

    for cond, group in sections:
        pl.when(cond)(lambda group=group: sent(group))


def shards(matrix):
    rows, cols = matrix.shape
    lower, upper = pl.pallas_call(
        kernel,
        out_shape=(jax.ShapeDtypeStruct((rows, NB), BF16), jax.ShapeDtypeStruct((rows, cols), BF16)),
        in_specs=[pl.BlockSpec(memory_space=pl.ANY)],
        out_specs=(pl.BlockSpec(memory_space=pltpu.VMEM), pl.BlockSpec(memory_space=pltpu.VMEM)),
        scratch_shapes=[
            pltpu.VMEM((rows, cols), F32),
            pltpu.VMEM((NB, NB), F32),
            pltpu.SemaphoreType.DMA((2,)),
            pltpu.SemaphoreType.DMA((200,)),
            pltpu.SemaphoreType.DMA((CHUNKS,)),
            pltpu.SemaphoreType.DMA((3,)),
            pltpu.SemaphoreType.DMA,
            pltpu.SemaphoreType.DMA((3,)),
            pltpu.SemaphoreType.DMA,
            pltpu.SemaphoreType.DMA,
        ]
        + [pltpu.SemaphoreType.REGULAR] * 5,
        compiler_params=pltpu.CompilerParams(
            collective_id=0, has_side_effects=True, vmem_limit_bytes=24 * 1024 * 1024
        ),
    )(pltpu.with_memory_space_constraint(matrix, pltpu.HBM))
    return matrix - jnp.dot(lower, upper, preferred_element_type=F32)


def solution(mesh):
    return jax.shard_map(
        shards,
        mesh=mesh,
        in_specs=(P("row", "col"),),
        out_specs=P("row", "col"),
        check_vma=False,
    )
```

time: 39.9 us -> 36.6 us (0.917)
  the two profiles are of different devices: /device:TPU:481 before, /device:TPU:97 now
where the time goes in v4:
time: 36.6 us; the launch traced here: 36.4 us
  Pallas kernels  35.1 us (96%)
  matrix products  1.28 us (3%)
    pallas_call x1, Pallas kernels, shards(): pl.pallas_call(kernel, out_shape=(jax.ShapeDtypeStruct((rows, NB), BF16),...  35.1 us
    dot_general x1, matrix products, shards(): return matrix - jnp.dot(lower, upper, preferred_element_type=F32)  1.28 us

profile of v4, /device:TPU:97, one launch (start us, length us, event | category | flops | bytes accessed | tf_op | source)
XLA Modules:
  0.0 36.4 jit_solution(16189110890413686726)
XLA Ops:
  0.0 0.0 copy-start
  0.0 35.1 %shard_map.17 = (bf16[256,256]{1,0:T(8,128)(2,1)S(1)}, bf16[256,1024]{1,0:T(8,128)(2,1)S(1)}) custom-call(f32[256,1024]{1,0:T(8,128)} %m_hbm.1), custom_call_target="tpu_custom_call" | custom-call | tf_op jit(solution)/shard_map/pallas_call | solution.py:353
  35.1 0.0 copy-done
  35.2 1.3 %convolution_subtract_fusion = f32[256,1024]{1,0:T(8,128)} fusion(f32[256,1024]{1,0:T(8,128)S(1)} %copy-done, bf16[256,256]{1,0:T(8,128)(2,1)S(1)} %get-tuple-element.7, bf16[256,1024]{1,0:T(8,128)(2,1)S(1)} %get-tuple-element.8), kind=kOutput, calls=%fused_computation | convolution fusion | flops 134479872 | bytes 2752512 | tf_op jit(solution)/shard_map/dot_general | solution.py:375
Async XLA Ops:
  0.0 35.1 %copy-start = (f32[256,1024]{1,0:T(8,128)S(1)}, f32[256,1024]{1,0:T(8,128)}, u32[]{:S(2)}) copy-start(f32[256,1024]{1,0:T(8,128)} %m_hbm.1) | copy-start | bytes 3145732

commit v5 on v4

--- a/solution.py
+++ b/solution.py
@@ -45,8 +45,8 @@
     return down * (first + (second + product(parts, split(second))))
 
 
-def kernel(m_hbm, l_ref, u_ref, m_ref, x_buf, m_sem, send_sem, own_sem, ux_sem, xz_sem, xx_sem, ly_sem, ls_sem,
-           ready_x, ready_y, ready_z, ready_w, ready_v):
+def kernel(m_hbm, l_ref, u_ref, m_ref, x_buf, m_sem, send_sem, own_sem, ux_sem, xz_sem, xx_sem, mc_sem, ls_sem,
+           ready_x, ready_y, ready_z, ready_w):
     row, col = lax.axis_index("row"), lax.axis_index("col")
     z, x = lax.div(row, NX), lax.rem(row, NX)
     y, core = lax.div(col, 2), lax.rem(col, 2)
@@ -54,10 +54,11 @@
     quarter = rows // NX
     chunk = quarter // CHUNKS
     piece = NB // NX
-    half = NB // 2
     top = row == 0
     below = row != 0
     first_col = col == 0
+    even = core == 0
+    mirror = even & (y != 0)
     other_col = col != 0
     root = top & first_col
     bottom = z == 0
@@ -70,10 +71,11 @@
     first_hub = first_col & hub
     other_hub = other_col & hub
     down_u = [(chain, z + 2), (chain, z + 1)] + [(other_hub, to) for to in (12, 14, 11, 15)]
-    down_x = (
-        [(source, to) for to in range(1, NEAR + 1)] + [(relay, 7), (relay, 8)]
-        + [(first_hub, to) for to in (9, 14, 10, 15, 11, 12)]
-    )
+    down_x = [
+        ((source | first_hub | relay) if i < 2 else (source | first_hub),
+         jnp.where(source, i + 1, jnp.where(relay, 7 + i, to)))
+        for i, to in enumerate((9, 14, 10, 15, 11, 12))
+    ]
     parent_z = jnp.where(
         first_col,
         jnp.where(z <= NEAR, 0, jnp.where(z < 9, 4, HUB)),
@@ -86,6 +88,7 @@
         return z * NX + lax.rem(x + j, NX)
 
     from_root_x = bottom & (x != 0) & first_col
+    from_root_y = top & mirror
     from_root_z = (z > 0) & (z <= NEAR) & (x == 0) & first_col
     by_parent = (z > 0) & jnp.logical_not(from_root_z)
 
@@ -116,7 +119,7 @@
 
     @pl.when(usual)
     def _():
-        signal(from_root_x | from_root_z, barrier, (0, 0))
+        signal(from_root_x | from_root_y | from_root_z, barrier, (0, 0))
         for j in (1, 2, 3):
             signal(x + j < NX, barrier, (row + j, col))
         for cond, to in down_u + down_x:
@@ -124,16 +127,14 @@
 
     @pl.when(below & first_col)
     def _():
-        for k in range(2, 2 * NY):
-            signal(None, barrier, (row, k))
-
-    signal(below & (y == 2), barrier, (row, 8 + core))
+        for k in range(1, NY):
+            signal(None, barrier, (row, 2 * k))
 
     pl.semaphore_wait(
         barrier,
-        jnp.where(root, NX - 1 + NEAR,
+        jnp.where(root, NX - 1 + NEAR + NY - 1,
                   one(paired) + one(top & (col == 1)) + x - one(from_root_x) + one(by_parent)
-                  + one(below & (y != 0)) + one(below & (y == 4))),
+                  + one(below & mirror)),
     )
 
     @pl.when(usual)
@@ -142,8 +143,7 @@
             signal((x >= j) & jnp.logical_not(from_root_x & (x == j)), ready_x, (row - j, col))
         signal(by_parent & jnp.logical_not(hub), ready_z, (parent_z * NX + x, col))
         signal(hub, ready_w, (x, col))
-        signal(below & (y != 0), ready_y, (row, 0))
-        signal(below & (y == 4), ready_v, (row, 4 + core))
+        signal(below & mirror, ready_y, (row, 0))
 
     sections = []
     used = [0]
@@ -225,6 +225,16 @@
     def _():
         narrow.wait()
 
+    def sent(group):
+        for only, part, spot in group:
+            gone = lambda part=part, spot=spot: arrived(part(), send_sem.at[spot])
+            gone() if only is None else pl.when(only)(gone)
+
+    def flush():
+        for cond, group in sections:
+            pl.when(cond)(lambda group=group: sent(group))
+        sections.clear()
+
     def start(send):
         x_buf[...] = inverse_of(m_ref[:, :NB])
         for q in (2, 1, 3):
@@ -238,6 +248,15 @@
         columns = col * cols + lax.broadcasted_iota(jnp.int32, (rows, cols), 1)
         u_ref[...] = jnp.where(columns < NB, 0.0, m_ref[...]).astype(BF16)
         l_ref[...] = jnp.zeros((rows, NB), BF16)
+
+    columns_here = lambda: m_ref.at[:, pl.ds(0, NB)]
+
+    def to_mirrors(send):
+        pl.semaphore_wait(ready_y, NY - 1)
+        for k in (4, 5, 3, 6, 2, 7, 1):
+            send(columns_here, mc_sem, (row, 2 * k))
+
+    section(first_col & below, to_mirrors)
 
     wait_for(usual & (x != NX - 1), ready_x, NX - 1 - x)
     wait_for(usual & (children > 0), ready_z, children)
@@ -253,6 +272,16 @@
 
     section(bottom & other_col, last(0))
 
+    def finish(first):
+        for j in (1, 2, 3):
+            arrived(u_quarter(lax.rem(x + NX - j, NX), first), ux_sem.at[j - 1])
+
+    pl.when(below & other_col)(lambda: finish(0))
+    later = sections[:2]
+    del sections[:2]
+    flush()
+    sections.extend(later)
+
     def inverse_rows(send):
         @pl.when(below)
         def _():
@@ -260,12 +289,21 @@
             arrived(x_part(x), xz_sem)
 
         mine = lambda: x_part(x)
+        for (cond, to), ys in zip(down_x, ((1, 7), (2, 6), (3, 5), (4,), (), ())):
+            for k in ys:
+                send(mine, xz_sem, (row, 2 * k))
+            send(mine, xz_sem, (to * NX + x, 0), cond)
         for j in (2, 1, 3):
             send(mine, xx_sem.at[j - 1], (at_x(j), 0), not_back[j - 1])
-        for cond, to in down_x:
-            send(mine, xz_sem, (to * NX + x, 0), cond)
 
     section(first_col, inverse_rows)
+
+    def mirror_rows(send):
+        arrived(x_part(x), xz_sem)
+        for j in (2, 1, 3):
+            send(lambda: x_part(x), xx_sem.at[j - 1], (at_x(j), col), not_back[j - 1])
+
+    section(mirror, mirror_rows)
 
     def scatter_first(send):
         for k in range(2):
@@ -279,22 +317,6 @@
         send(lambda: x_part(x), xz_sem, (HUB * NX + x, 0))
 
     section(first_col & bottom, to_hub)
-
-    def l_part(h):
-        return l_ref.at[pl.ds(pl.multiple_of(h * half, half), half), :]
-
-    def make_lower(send):
-        left = split(m_ref[:, :NB])
-        for j in (1, 2, 3):
-            arrived(x_part(lax.rem(x + NX - j, NX)), xx_sem.at[j - 1])
-        l_ref[...] = product(left, split(x_buf[...])).astype(BF16)
-        pl.semaphore_wait(ready_y, 2 * NY - 2)
-        for k in (2, 6, 3, 7, 1, 5):
-            for h in (0, 1):
-                send(lambda h=h: l_part(h), ly_sem, (row, k * 2 + h))
-        send(lambda: l_ref, ly_sem, (row, 1))
-
-    section(first_col & below, make_lower)
 
     def spread_first(send):
         for k in range(2):
@@ -310,42 +332,26 @@
 
     section(first_col, spread_first)
 
-    passes = y == 2
-
-    def relay_lower(send):
-        arrived(l_part(core), ly_sem)
-
-        @pl.when(passes)
+    def make_lower(send):
+        @pl.when(mirror)
         def _():
-            pl.semaphore_wait(ready_v, 1)
-
-        send(lambda: l_part(core), ly_sem, (row, 8 + core), passes)
-        send(lambda: l_part(core), ls_sem, (row, y * 2 + 1 - core))
-
-    section(below & (y != 0), relay_lower)
-
-    def finish(first):
+            arrived(columns_here(), mc_sem)
+
+        left = split(m_ref[:, :NB])
         for j in (1, 2, 3):
-            arrived(u_quarter(lax.rem(x + NX - j, NX), first), ux_sem.at[j - 1])
-
-    pl.when(below & other_col)(lambda: finish(0))
+            arrived(x_part(lax.rem(x + NX - j, NX)), xx_sem.at[j - 1])
+        l_ref[...] = product(left, split(x_buf[...])).astype(BF16)
+        send(lambda: l_ref, ls_sem, (row, col + 1))
+
+    section(below & even, make_lower)
+
     pl.when(below & first_col)(lambda: finish(NB))
 
-    @pl.when(below & (y != 0))
-    def _():
-        arrived(l_part(1 - core), ls_sem)
-
-    @pl.when(below & (col == 1))
-    def _():
-        arrived(l_ref, ly_sem)
-
-    def sent(group):
-        for only, part, spot in group:
-            gone = lambda part=part, spot=spot: arrived(part(), send_sem.at[spot])
-            gone() if only is None else pl.when(only)(gone)
-
-    for cond, group in sections:
-        pl.when(cond)(lambda group=group: sent(group))
+    @pl.when(below & (core == 1))
+    def _():
+        arrived(l_ref, ls_sem)
+
+    flush()
 
 
 def shards(matrix):
@@ -367,7 +373,7 @@
             pltpu.SemaphoreType.DMA,
             pltpu.SemaphoreType.DMA,
         ]
-        + [pltpu.SemaphoreType.REGULAR] * 5,
+        + [pltpu.SemaphoreType.REGULAR] * 4,
         compiler_params=pltpu.CompilerParams(
             collective_id=0, has_side_effects=True, vmem_limit_bytes=24 * 1024 * 1024
         ),

time: 36.6 us -> 35.8 us (0.978)
  the two profiles are of different devices: /device:TPU:97 before, /device:TPU:737 now
where the time goes in v5:
time: 35.8 us; the launch traced here: 35.6 us
  Pallas kernels  34.3 us (96%)
  matrix products  1.28 us (4%)
    pallas_call x1, Pallas kernels, shards(): pl.pallas_call(kernel, out_shape=(jax.ShapeDtypeStruct((rows, NB), BF16),...  34.3 us
    dot_general x1, matrix products, shards(): return matrix - jnp.dot(lower, upper, preferred_element_type=F32)  1.28 us

profile of v5, /device:TPU:737, one launch (start us, length us, event | category | flops | bytes accessed | tf_op | source)
XLA Modules:
  0.0 35.6 jit_solution(14205384031874353935)
XLA Ops:
  0.0 0.0 copy-start
  0.0 34.3 %shard_map.17 = (bf16[256,256]{1,0:T(8,128)(2,1)S(1)}, bf16[256,1024]{1,0:T(8,128)(2,1)S(1)}) custom-call(f32[256,1024]{1,0:T(8,128)} %m_hbm.1), custom_call_target="tpu_custom_call" | custom-call | tf_op jit(solution)/shard_map/pallas_call | solution.py:359
  34.3 0.0 copy-done
  34.3 1.3 %convolution_subtract_fusion = f32[256,1024]{1,0:T(8,128)} fusion(f32[256,1024]{1,0:T(8,128)S(1)} %copy-done, bf16[256,256]{1,0:T(8,128)(2,1)S(1)} %get-tuple-element.7, bf16[256,1024]{1,0:T(8,128)(2,1)S(1)} %get-tuple-element.8), kind=kOutput, calls=%fused_computation | convolution fusion | flops 134479872 | bytes 2752512 | tf_op jit(solution)/shard_map/dot_general | solution.py:381
Async XLA Ops:
  0.0 34.3 %copy-start = (f32[256,1024]{1,0:T(8,128)S(1)}, f32[256,1024]{1,0:T(8,128)}, u32[]{:S(2)}) copy-start(f32[256,1024]{1,0:T(8,128)} %m_hbm.1) | copy-start | bytes 3145732

commit v6 on v5

--- a/solution.py
+++ b/solution.py
@@ -81,8 +81,8 @@
         jnp.where(z <= NEAR, 0, jnp.where(z < 9, 4, HUB)),
         jnp.where(z > CHAIN + 2, HUB, jnp.where(lax.rem(z, 2) == 0, z - 2, z - 1)),
     )
-    children = (jnp.where(source, NEAR, 0) + jnp.where(relay, 2, 0) + jnp.where(first_hub, 6, 0)
-                + jnp.where(chain, 2, 0) + jnp.where(other_hub, 4, 0))
+    children = (jnp.where(source, NEAR, 0) + jnp.where(relay, 2, 0) + jnp.where(first_hub, 4, 0)
+                + jnp.where(chain | other_hub, 2, 0))
 
     def at_x(j):
         return z * NX + lax.rem(x + j, NX)
@@ -90,7 +90,8 @@
     from_root_x = bottom & (x != 0) & first_col
     from_root_y = top & mirror
     from_root_z = (z > 0) & (z <= NEAR) & (x == 0) & first_col
-    by_parent = (z > 0) & jnp.logical_not(from_root_z)
+    from_hub = (z == HUB - 1) | (z == HUB - 2)
+    by_parent = (z > 0) & jnp.logical_not(from_root_z | from_hub)
 
     narrow = pltpu.make_async_copy(m_hbm.at[:, pl.ds(0, NB)], m_ref.at[:, pl.ds(0, NB)], m_sem.at[0])
     rest = pl.ds(NB, cols - NB)
@@ -123,7 +124,9 @@
         for j in (1, 2, 3):
             signal(x + j < NX, barrier, (row + j, col))
         for cond, to in down_u + down_x:
-            signal(cond, barrier, (to * NX + x, col))
+            nearest = hub & ((to == HUB - 1) | (to == HUB - 2))
+            signal(cond & jnp.logical_not(nearest), barrier, (to * NX + x, col))
+        signal(from_hub, barrier, (HUB * NX + x, col))
 
     @pl.when(below & first_col)
     def _():
@@ -134,7 +137,7 @@
         barrier,
         jnp.where(root, NX - 1 + NEAR + NY - 1,
                   one(paired) + one(top & (col == 1)) + x - one(from_root_x) + one(by_parent)
-                  + one(below & mirror)),
+                  + one(below & mirror) + jnp.where(hub, 2, 0)),
     )
 
     @pl.when(usual)
@@ -198,7 +201,14 @@
                     send(lambda q=q, k=k: u_part(q, k, first), own_sem.at[k], (q, col))
         return body
 
-    not_back = [at_x(j) != 0 for j in (1, 2, 3)]
+    over_x = [
+        (j, at_x(j), at_x(j) != 0)
+        for j in (
+            jnp.where(x == 0, 2, NX - x),
+            jnp.where((x == 0) | (x == 2), 1, 2),
+            jnp.where(x == 1, 1, 3),
+        )
+    ]
 
     def spread_u(first):
         def body(send):
@@ -209,8 +219,8 @@
                 def _():
                     arrived(part(), own_sem.at[k])
 
-                for j in (2, 1, 3):
-                    send(part, ux_sem.at[j - 1], (at_x(j), col), not_back[j - 1])
+                for j, to, allowed in over_x:
+                    send(part, ux_sem.at[j - 1], (to, col), allowed)
                 for further, to in down_u:
                     send(part, own_sem.at[k], (to * NX + x, col), further)
         return body
@@ -272,6 +282,14 @@
 
     section(bottom & other_col, last(0))
 
+    def mirror_rows(send):
+        arrived(x_part(x), xz_sem)
+        for j, to, allowed in over_x:
+            send(lambda: x_part(x), xx_sem.at[j - 1], (to, col), allowed)
+
+    section(mirror, mirror_rows)
+
+
     def finish(first):
         for j in (1, 2, 3):
             arrived(u_quarter(lax.rem(x + NX - j, NX), first), ux_sem.at[j - 1])
@@ -293,17 +311,10 @@
             for k in ys:
                 send(mine, xz_sem, (row, 2 * k))
             send(mine, xz_sem, (to * NX + x, 0), cond)
-        for j in (2, 1, 3):
-            send(mine, xx_sem.at[j - 1], (at_x(j), 0), not_back[j - 1])
+        for j, to, allowed in over_x:
+            send(mine, xx_sem.at[j - 1], (to, 0), allowed)
 
     section(first_col, inverse_rows)
-
-    def mirror_rows(send):
-        arrived(x_part(x), xz_sem)
-        for j in (2, 1, 3):
-            send(lambda: x_part(x), xx_sem.at[j - 1], (at_x(j), col), not_back[j - 1])
-
-    section(mirror, mirror_rows)
 
     def scatter_first(send):
         for k in range(2):
@@ -324,8 +335,8 @@
             def _():
                 arrived(first_part(x, k), own_sem.at[k])
 
-            for j in (2, 1, 3):
-                send(lambda k=k: first_part(x, k), ux_sem.at[j - 1], (at_x(j), col), not_back[j - 1])
+            for j, to, allowed in over_x:
+                send(lambda k=k: first_part(x, k), ux_sem.at[j - 1], (to, col), allowed)
         for cond, to in down_x + [(bottom, HUB)]:
             for k in range(2):
                 send(lambda k=k: first_part(x, k), own_sem.at[k], (to * NX + x, col), cond)

time: 35.8 us -> 35.2 us (0.983)
  the two profiles are of different devices: /device:TPU:737 before, /device:TPU:865 now
where the time goes in v6:
time: 35.2 us; the launch traced here: 35.1 us
  Pallas kernels  33.8 us (96%)
  matrix products  1.28 us (4%)
    pallas_call x1, Pallas kernels, shards(): pl.pallas_call(kernel, out_shape=(jax.ShapeDtypeStruct((rows, NB), BF16),...  33.8 us
    dot_general x1, matrix products, shards(): return matrix - jnp.dot(lower, upper, preferred_element_type=F32)  1.28 us

profile of v6, /device:TPU:865, one launch (start us, length us, event | category | flops | bytes accessed | tf_op | source)
XLA Modules:
  0.0 35.1 jit_solution(4630675708125678793)
XLA Ops:
  0.0 0.0 copy-start
  0.0 33.8 %shard_map.17 = (bf16[256,256]{1,0:T(8,128)(2,1)S(1)}, bf16[256,1024]{1,0:T(8,128)(2,1)S(1)}) custom-call(f32[256,1024]{1,0:T(8,128)} %m_hbm.1), custom_call_target="tpu_custom_call" | custom-call | tf_op jit(solution)/shard_map/pallas_call | solution.py:370
  33.8 0.0 copy-done
  33.8 1.3 %convolution_subtract_fusion = f32[256,1024]{1,0:T(8,128)} fusion(f32[256,1024]{1,0:T(8,128)S(1)} %copy-done, bf16[256,256]{1,0:T(8,128)(2,1)S(1)} %get-tuple-element.7, bf16[256,1024]{1,0:T(8,128)(2,1)S(1)} %get-tuple-element.8), kind=kOutput, calls=%fused_computation | convolution fusion | flops 134479872 | bytes 2752512 | tf_op jit(solution)/shard_map/dot_general | solution.py:392
Async XLA Ops:
  0.0 33.8 %copy-start = (f32[256,1024]{1,0:T(8,128)S(1)}, f32[256,1024]{1,0:T(8,128)}, u32[]{:S(2)}) copy-start(f32[256,1024]{1,0:T(8,128)} %m_hbm.1) | copy-start | bytes 3145732
